TPU v7x, 32 devices: a whole 2x2x4 slice. The times are simulated.
32 devices in a mesh: dp: 4 (over z), expert: 4 (over y, x), tensor: 2 (over core).
Axes of the slice: x: 2, y: 2, z: 4, core: 2. Of those that a mesh axis runs over, the one named last changes fastest.
Arguments:
- tokens: bfloat16 [8192, 1536], P(('dp', 'tensor')), may hold values from -6 to 6
- deal: int32 [16], P(('dp', 'tensor')), may hold values from 0 to 15, as said below
- lengths: int32 [16], P(('dp', 'tensor')), may hold values from 256 to 512, as said below
- priority: int32 [8192], P(('dp', 'tensor')), may hold values from 0 to 511, as said below
- routes: int32 [8192, 2], P(('dp', 'tensor')), may hold values from 0 to 15, all different within a row
- gain_attn: bfloat16 [1536], P(('dp', 'tensor')), may hold values from 0.5 to 1.5
- w_query: bfloat16 [1536, 1536], P(('dp', 'tensor'), 'expert'), may hold values from -0.15625 to 0.15625
- w_key: bfloat16 [1536, 512], P(('dp', 'tensor'), 'expert'), may hold values from -0.15625 to 0.15625
- w_value: bfloat16 [1536, 512], P(('dp', 'tensor'), 'expert'), may hold values from -0.15625 to 0.15625
- w_out: bfloat16 [1536, 1536], P('expert', ('dp', 'tensor')), may hold values from -0.625 to 0.625
- gain_ffn: bfloat16 [1536], P(('dp', 'tensor')), may hold values from 0.5 to 1.5
- w_router: bfloat16 [1536, 16], P(('dp', 'tensor')), may hold values from -0.15625 to 0.15625
- w_gate: bfloat16 [16, 1536, 1024], P('expert', 'dp', 'tensor'), may hold values from -0.15625 to 0.15625
- w_up: bfloat16 [16, 1536, 1024], P('expert', 'dp', 'tensor'), may hold values from -0.15625 to 0.15625
- w_down: bfloat16 [16, 1024, 1536], P('expert', 'tensor', 'dp'), may hold values from -1.5 to 1.5
- cotangent: bfloat16 [8192, 1536], P(('dp', 'tensor')), may hold values from -6 to 6
Outputs:
- output: bfloat16 [8192, 1536], P(('dp', 'tensor'))
- d_tokens: bfloat16 [8192, 1536], P(('dp', 'tensor'))
- d_gain_attn: float32 [1536], P(('dp', 'tensor'))
- d_w_query: float32 [1536, 1536], P(('dp', 'tensor'), 'expert')
- d_w_key: float32 [1536, 512], P(('dp', 'tensor'), 'expert')
- d_w_value: float32 [1536, 512], P(('dp', 'tensor'), 'expert')
- d_w_out: float32 [1536, 1536], P('expert', ('dp', 'tensor'))
- d_gain_ffn: float32 [1536], P(('dp', 'tensor'))
- d_w_router: float32 [1536, 16], P(('dp', 'tensor'))
- d_w_gate: float32 [16, 1536, 1024], P('expert', 'dp', 'tensor')
- d_w_up: float32 [16, 1536, 1024], P('expert', 'dp', 'tensor')
- d_w_down: float32 [16, 1024, 1536], P('expert', 'tensor', 'dp')
Inputs may be any that keep to these rules, and one draw needn't show every extreme that they name: A permutation of the places; for each micro-batch m there is one number k_m, 1 to 7, such that deal[o * 2 + m] = (o xor k_m) * 2 + m for every o. Each sequence's live tokens are its first lengths slots; in every draw some sequence has all 512 slots live. `priority`: within each place's 512 rows, a permutation of 0 to 511.
All inputs are finite; a program needn't handle non-finite values.
Results may differ from a plain program's by a relative error of at most 0.03.
Values may be sent and summed in bfloat16 or wider, within the bound.
No kernel may reach another device: no remote copies, remote signals or barrier semaphores. Data moves between devices by JAX's collectives and lax.ppermute only.
A program may use at most 256 MiB of HBM per device.

v0:
```python
import math

import jax
import jax.numpy as jnp
from jax import lax
from jax.sharding import PartitionSpec as P

D = 1536
HEADS = 24
KV_HEADS = 8
HEAD_DIM = 64
EXPERTS = 16
TOP = 2
SEQ_LEN = 512
MICRO = 2
CAP = 80


norm_epsilon = 1e-05
masked_score = -1e30


def partner_2(block, axis, distance):
    count = lax.axis_size(axis)
    route = []
    for low in range(count):
        high = low | 1 << distance
        if high != low and high < count:
            route += [(low, high), (high, low)]
    return lax.ppermute(block, axis, route)


def slotting(length_one, priority_one, route_rows):
    count = priority_one.shape[0]
    positions = jnp.arange(count, dtype=jnp.int32)
    live_rows = positions < length_one
    inverse = jnp.zeros((count,), jnp.int32).at[priority_one].set(positions)
    ranked = route_rows[inverse].reshape(-1)
    ranked_live = jnp.repeat(live_rows[inverse], TOP)
    table = (
        (ranked[:, None] == jnp.arange(EXPERTS, dtype=jnp.int32)[None, :]) & ranked_live[:, None]
    ).astype(jnp.int32)
    before = jnp.cumsum(table, axis=0) - table
    place_ranked = jnp.sum(before * table, axis=1)
    place = place_ranked.reshape(count, TOP)[priority_one]
    kept_pair = live_rows[:, None] & (place < CAP)
    slot_index = jnp.where(kept_pair, route_rows * CAP + place, EXPERTS * CAP)
    pair_ids = jnp.arange(count * TOP, dtype=jnp.int32)
    slot_pair = (
        jnp.full((EXPERTS * CAP + 1,), count * TOP, jnp.int32)
        .at[slot_index.reshape(-1)]
        .set(pair_ids)
    )
    return (slot_index, slot_pair[: EXPERTS * CAP])


def move_rows(stacked, mask_value, bit_count):
    for bit_number in range(bit_count):
        partner = partner_2(stacked, ("dp", "tensor"), bit_number)
        taken = jnp.bitwise_and(jnp.right_shift(mask_value, bit_number), 1) == 1
        stacked = jnp.where(taken, partner, stacked)
    return stacked


def rms_scale(values):
    return lax.rsqrt(jnp.mean(values * values, axis=-1, keepdims=True) + norm_epsilon)


def norm_back(values, scale_rows, grad_in, gain_rows):
    weighted = grad_in * gain_rows
    inner_sum = jnp.mean(values * weighted, axis=-1, keepdims=True)
    return scale_rows * weighted - values * (scale_rows * scale_rows * scale_rows) * inner_sum


def contract_rows(left, right):
    return lax.dot_general(
        left, right, (((0,), (0,)), ((), ())), preferred_element_type=jnp.float32
    )


def times_transpose(left, right):
    return lax.dot_general(
        left, right, (((1,), (1,)), ((), ())), preferred_element_type=jnp.float32
    )


def score_block(query_block, key_heads, row_first, length_one, scale_value):
    block_rows = query_block.shape[0]
    scores = (
        jnp.einsum("qkgd,skd->kgqs", query_block, key_heads, preferred_element_type=jnp.float32)
        * scale_value
    )
    query_pos = row_first + jnp.arange(block_rows, dtype=jnp.int32)
    key_pos = jnp.arange(key_heads.shape[0], dtype=jnp.int32)
    allowed = (key_pos[None, :] <= query_pos[:, None]) & (key_pos[None, :] < length_one)
    return (jnp.where(allowed, scores, masked_score), allowed)


def local(
    tokens,
    deal,
    lengths,
    priority,
    routes,
    gain_attn,
    w_query,
    w_key,
    w_value,
    w_out,
    gain_ffn,
    w_router,
    w_gate,
    w_up,
    w_down,
    cotangent,
):
    gain_one, query_weight, key_weight, value_weight, out_weight, gain_two, router_weight = (
        lax.all_gather(gain_attn, ("dp", "tensor"), axis=0, tiled=True),
        lax.all_gather(w_query, ("dp", "tensor"), axis=0, tiled=True),
        lax.all_gather(w_key, ("dp", "tensor"), axis=0, tiled=True),
        lax.all_gather(w_value, ("dp", "tensor"), axis=0, tiled=True),
        lax.all_gather(w_out, ("dp", "tensor"), axis=1, tiled=True),
        lax.all_gather(gain_ffn, ("dp", "tensor"), axis=0, tiled=True),
        lax.all_gather(w_router, ("dp", "tensor"), axis=0, tiled=True),
    )
    gate_weight, up_weight, down_weight = (
        lax.all_gather(w_gate, "dp", axis=1, tiled=True),
        lax.all_gather(w_up, "dp", axis=1, tiled=True),
        lax.all_gather(w_down, "dp", axis=2, tiled=True),
    )
    owner_index = lax.axis_index(("dp", "tensor"))
    bit_count = lax.axis_size(("dp", "tensor")).bit_length() - 1
    expert_count = lax.axis_size("expert")
    expert_index = lax.axis_index("expert")
    local_experts = EXPERTS // expert_count
    local_heads = HEADS // expert_count
    local_kv = KV_HEADS // expert_count
    groups_per = HEADS // KV_HEADS
    scale_value = 1.0 / math.sqrt(HEAD_DIM)
    block_rows = min(512, SEQ_LEN)
    block_count = SEQ_LEN // block_rows
    gain_onef = gain_one.astype(jnp.float32)
    gain_twof = gain_two.astype(jnp.float32)
    offset = expert_index * (local_experts * CAP)
    attn_sums = [
        jnp.zeros(part_array.shape, jnp.float32)
        for part_array in (
            gain_one,
            query_weight,
            key_weight,
            value_weight,
            out_weight,
            gain_two,
            router_weight,
        )
    ]
    expert_sums = [
        jnp.zeros(part_array.shape, jnp.float32)
        for part_array in (gate_weight, up_weight, down_weight)
    ]
    result_rows = []
    grad_rows_out = []
    for micro_index in range(MICRO):
        row_start = micro_index * SEQ_LEN
        row_end = row_start + SEQ_LEN
        mask_value = jnp.bitwise_xor(deal[micro_index] // MICRO, owner_index)
        arriving = move_rows(
            jnp.stack([tokens[row_start:row_end], cotangent[row_start:row_end]], axis=0),
            mask_value,
            bit_count,
        )
        inputs = arriving[0].astype(jnp.float32)
        length_one = lengths[micro_index]
        route_rows = routes[row_start:row_end]
        scale_one = rms_scale(inputs)
        normed_one = (inputs * scale_one * gain_onef).astype(jnp.bfloat16)
        query_rows = jnp.dot(normed_one, query_weight, preferred_element_type=jnp.float32).astype(
            jnp.bfloat16
        )
        key_rows = jnp.dot(normed_one, key_weight, preferred_element_type=jnp.float32).astype(
            jnp.bfloat16
        )
        value_rows = jnp.dot(normed_one, value_weight, preferred_element_type=jnp.float32).astype(
            jnp.bfloat16
        )
        query_heads = query_rows.reshape(SEQ_LEN, local_kv, groups_per, HEAD_DIM)
        key_heads = key_rows.reshape(SEQ_LEN, local_kv, HEAD_DIM)
        value_heads = value_rows.reshape(SEQ_LEN, local_kv, HEAD_DIM)

        def forward_block(block_index):
            row_first = block_index * block_rows
            scores, allowed = score_block(
                query_heads, key_heads, row_first, length_one, scale_value
            )
            highest = jnp.max(scores, axis=-1, keepdims=True)
            expsum = jnp.exp(scores - highest)
            totals = jnp.sum(expsum, axis=-1, keepdims=True)
            weights = (expsum / totals).astype(jnp.bfloat16)
            mixed_block = jnp.einsum(
                "kgqs,skd->qkgd", weights, value_heads, preferred_element_type=jnp.float32
            )
            return (mixed_block.astype(jnp.bfloat16), highest + jnp.log(totals))

        mixed_blocks, log_totals = lax.map(forward_block, jnp.arange(block_count, dtype=jnp.int32))
        mixed_rows = mixed_blocks.reshape(SEQ_LEN, local_heads * HEAD_DIM)
        attn_part = jnp.dot(mixed_rows, out_weight, preferred_element_type=jnp.float32)
        attn_part = attn_part.astype(jnp.bfloat16).astype(jnp.float32)
        attention = lax.psum(attn_part.astype(jnp.bfloat16), "expert").astype(jnp.float32)
        hidden_one = inputs + attention
        scale_two = rms_scale(hidden_one)
        normed_two = (hidden_one * scale_two * gain_twof).astype(jnp.bfloat16)
        logits = jnp.dot(normed_two, router_weight, preferred_element_type=jnp.float32)
        router = jax.nn.softmax(logits, axis=-1)
        gate_values = jnp.take_along_axis(router, route_rows, axis=1)
        slot_index, slot_pair = slotting(length_one, priority[row_start:row_end], route_rows)
        local_pair = lax.dynamic_slice_in_dim(slot_pair, offset, local_experts * CAP, 0)
        padded_two = jnp.concatenate([normed_two, jnp.zeros((1, D), jnp.bfloat16)], axis=0)
        slot_rows = padded_two[local_pair // TOP].reshape(local_experts, CAP, D)
        all_slots = lax.all_gather(slot_rows, "tensor", axis=1, tiled=True)
        gate_in = jnp.einsum(
            "ecd,edf->ecf", all_slots, gate_weight, preferred_element_type=jnp.float32
        )
        up_in = jnp.einsum("ecd,edf->ecf", all_slots, up_weight, preferred_element_type=jnp.float32)
        activated = jax.nn.silu(gate_in)
        hidden = (activated * up_in).astype(jnp.bfloat16)
        partial_out = jnp.einsum(
            "ecf,efd->ecd", hidden, down_weight, preferred_element_type=jnp.float32
        )
        expert_out = lax.psum_scatter(
            partial_out.astype(jnp.bfloat16), "tensor", scatter_dimension=1, tiled=True
        ).astype(jnp.float32)
        owner_group = route_rows // local_experts
        local_slot = jnp.where(
            (owner_group == expert_index) & (slot_index < EXPERTS * CAP),
            slot_index - offset,
            local_experts * CAP,
        )
        flat_out = jnp.concatenate(
            [expert_out.reshape(local_experts * CAP, D), jnp.zeros((1, D), jnp.float32)], axis=0
        )
        picked = flat_out[local_slot]
        moe_part = jnp.sum(picked * gate_values[:, :, None], axis=1)
        moe_part = moe_part.astype(jnp.bfloat16).astype(jnp.float32)
        expert_mix = lax.psum(moe_part.astype(jnp.bfloat16), "expert").astype(jnp.float32)
        result_owner = (hidden_one + expert_mix).astype(jnp.bfloat16)
        grad_out = arriving[1].astype(jnp.float32)
        gates_flat = jnp.concatenate(
            [gate_values.reshape(-1), jnp.zeros((1,), jnp.float32)], axis=0
        )
        grad_padded = jnp.concatenate([grad_out, jnp.zeros((1, D), jnp.float32)], axis=0)
        grad_slot = (gates_flat[local_pair][:, None] * grad_padded[local_pair // TOP]).astype(
            jnp.bfloat16
        )
        grad_slot = grad_slot.reshape(local_experts, CAP, D)
        all_grads = lax.all_gather(grad_slot, "tensor", axis=1, tiled=True)
        grad_down = jnp.einsum(
            "ecf,ecd->efd", hidden, all_grads, preferred_element_type=jnp.float32
        )
        grad_hidden = jnp.einsum(
            "ecd,efd->ecf", all_grads, down_weight, preferred_element_type=jnp.float32
        )
        sigmoid_in = jax.nn.sigmoid(gate_in)
        grad_gate_in = (
            grad_hidden * up_in * (sigmoid_in * (1.0 + gate_in * (1.0 - sigmoid_in)))
        ).astype(jnp.bfloat16)
        grad_up_in = (grad_hidden * activated).astype(jnp.bfloat16)
        grad_wgate = jnp.einsum(
            "ecd,ecf->edf", all_slots, grad_gate_in, preferred_element_type=jnp.float32
        )
        grad_wup = jnp.einsum(
            "ecd,ecf->edf", all_slots, grad_up_in, preferred_element_type=jnp.float32
        )
        slot_terms = jnp.einsum(
            "ecf,edf->ecd", grad_gate_in, gate_weight, preferred_element_type=jnp.float32
        )
        slot_terms = slot_terms + jnp.einsum(
            "ecf,edf->ecd", grad_up_in, up_weight, preferred_element_type=jnp.float32
        )
        grad_slot_rows = lax.psum_scatter(
            slot_terms.astype(jnp.bfloat16), "tensor", scatter_dimension=1, tiled=True
        ).astype(jnp.float32)
        flat_grad = jnp.concatenate(
            [grad_slot_rows.reshape(local_experts * CAP, D), jnp.zeros((1, D), jnp.float32)], axis=0
        )
        grad_normed_part = jnp.sum(flat_grad[local_slot], axis=1)
        grad_gates_part = jnp.sum(picked * grad_out[:, None, :], axis=-1)
        grad_normed_two, grad_gates = (
            lax.psum(grad_normed_part.astype(jnp.bfloat16), "expert").astype(jnp.float32),
            lax.psum(grad_gates_part.astype(jnp.bfloat16), "expert").astype(jnp.float32),
        )
        choice_table = (
            route_rows[:, :, None] == jnp.arange(EXPERTS, dtype=jnp.int32)[None, None, :]
        ).astype(jnp.float32)
        grad_router_probs = jnp.sum(choice_table * grad_gates[:, :, None], axis=1)
        inner_sum = jnp.sum(router * grad_router_probs, axis=-1, keepdims=True)
        grad_logits = (router * (grad_router_probs - inner_sum)).astype(jnp.bfloat16)
        grad_router = contract_rows(normed_two, grad_logits)
        grad_normed_two = grad_normed_two + times_transpose(grad_logits, router_weight)
        grad_gain_two = jnp.sum(grad_normed_two * hidden_one * scale_two, axis=0)
        grad_hidden_one = grad_out + norm_back(hidden_one, scale_two, grad_normed_two, gain_twof)
        grad_branch = grad_hidden_one.astype(jnp.bfloat16)
        grad_wout = contract_rows(mixed_rows, grad_branch)
        grad_mixed = times_transpose(grad_branch, out_weight).astype(jnp.bfloat16)
        grad_mixed = grad_mixed.reshape(SEQ_LEN, local_kv, groups_per, HEAD_DIM)

        def backward_block(running, block_index):
            grad_keys, grad_values = running
            row_first = block_index * block_rows
            scores, allowed = score_block(
                query_heads, key_heads, row_first, length_one, scale_value
            )
            weights_full = jnp.where(allowed, jnp.exp(scores - log_totals[block_index]), 0.0)
            weights_low = weights_full.astype(jnp.bfloat16)
            grad_weights = jnp.einsum(
                "qkgd,skd->kgqs", grad_mixed, value_heads, preferred_element_type=jnp.float32
            )
            row_inner = jnp.sum(weights_full * grad_weights, axis=-1, keepdims=True)
            grad_scores = (weights_full * (grad_weights - row_inner)).astype(jnp.bfloat16)
            grad_query = (
                jnp.einsum(
                    "kgqs,skd->qkgd", grad_scores, key_heads, preferred_element_type=jnp.float32
                )
                * scale_value
            )
            grad_keys = (
                grad_keys
                + jnp.einsum(
                    "kgqs,qkgd->skd", grad_scores, query_heads, preferred_element_type=jnp.float32
                )
                * scale_value
            )
            grad_values = grad_values + jnp.einsum(
                "kgqs,qkgd->skd", weights_low, grad_mixed, preferred_element_type=jnp.float32
            )
            return ((grad_keys, grad_values), grad_query)

        start_pair = (
            jnp.zeros((SEQ_LEN, local_kv, HEAD_DIM), jnp.float32),
            jnp.zeros((SEQ_LEN, local_kv, HEAD_DIM), jnp.float32),
        )
        (grad_keys, grad_values), grad_query_blocks = lax.scan(
            backward_block, start_pair, jnp.arange(block_count, dtype=jnp.int32)
        )
        grad_query = grad_query_blocks.reshape(SEQ_LEN, local_heads * HEAD_DIM).astype(jnp.bfloat16)
        grad_keys = grad_keys.reshape(SEQ_LEN, local_kv * HEAD_DIM).astype(jnp.bfloat16)
        grad_values = grad_values.reshape(SEQ_LEN, local_kv * HEAD_DIM).astype(jnp.bfloat16)
        grad_wquery = contract_rows(normed_one, grad_query)
        grad_wkey = contract_rows(normed_one, grad_keys)
        grad_wvalue = contract_rows(normed_one, grad_values)
        norm_part = (
            times_transpose(grad_query, query_weight)
            + times_transpose(grad_keys, key_weight)
            + times_transpose(grad_values, value_weight)
        )
        grad_normed_one = lax.psum(norm_part.astype(jnp.bfloat16), "expert").astype(jnp.float32)
        grad_gain_one = jnp.sum(grad_normed_one * inputs * scale_one, axis=0)
        grad_inputs = grad_hidden_one + norm_back(inputs, scale_one, grad_normed_one, gain_onef)
        leaving = move_rows(
            jnp.stack([result_owner, grad_inputs.astype(jnp.bfloat16)], axis=0),
            mask_value,
            bit_count,
        )
        result_rows.append(leaving[0])
        grad_rows_out.append(leaving[1])
        attn_terms = (
            grad_gain_one,
            grad_wquery,
            grad_wkey,
            grad_wvalue,
            grad_wout,
            grad_gain_two,
            grad_router,
        )
        expert_terms = (grad_wgate, grad_wup, grad_down)
        attn_sums = [running_sum + new_term for running_sum, new_term in zip(attn_sums, attn_terms)]
        expert_sums = [
            running_sum + new_term for running_sum, new_term in zip(expert_sums, expert_terms)
        ]
    attn_sums = (
        lax.psum_scatter(attn_sums[0], ("dp", "tensor"), scatter_dimension=0, tiled=True),
        lax.psum_scatter(attn_sums[1], ("dp", "tensor"), scatter_dimension=0, tiled=True),
        lax.psum_scatter(attn_sums[2], ("dp", "tensor"), scatter_dimension=0, tiled=True),
        lax.psum_scatter(attn_sums[3], ("dp", "tensor"), scatter_dimension=0, tiled=True),
        lax.psum_scatter(attn_sums[4], ("dp", "tensor"), scatter_dimension=1, tiled=True),
        lax.psum_scatter(attn_sums[5], ("dp", "tensor"), scatter_dimension=0, tiled=True),
        lax.psum_scatter(attn_sums[6], ("dp", "tensor"), scatter_dimension=0, tiled=True),
    )
    expert_sums = (
        lax.psum_scatter(
            expert_sums[0].astype(jnp.bfloat16), "dp", scatter_dimension=1, tiled=True
        ).astype(jnp.float32),
        lax.psum_scatter(
            expert_sums[1].astype(jnp.bfloat16), "dp", scatter_dimension=1, tiled=True
        ).astype(jnp.float32),
        lax.psum_scatter(
            expert_sums[2].astype(jnp.bfloat16), "dp", scatter_dimension=2, tiled=True
        ).astype(jnp.float32),
    )
    result_all = jnp.concatenate(result_rows, axis=0)
    grads_all = jnp.concatenate(grad_rows_out, axis=0)
    return (
        result_all,
        grads_all,
        attn_sums[0],
        attn_sums[1],
        attn_sums[2],
        attn_sums[3],
        attn_sums[4],
        attn_sums[5],
        attn_sums[6],
        expert_sums[0],
        expert_sums[1],
        expert_sums[2],
    )


def solution(mesh):
    placed = (
        P(("dp", "tensor"), None),
        P(("dp", "tensor")),
        P(("dp", "tensor")),
        P(("dp", "tensor")),
        P(("dp", "tensor"), None),
        P(("dp", "tensor")),
        P(("dp", "tensor"), "expert"),
        P(("dp", "tensor"), "expert"),
        P(("dp", "tensor"), "expert"),
        P("expert", ("dp", "tensor")),
        P(("dp", "tensor")),
        P(("dp", "tensor"), None),
        P("expert", "dp", "tensor"),
        P("expert", "dp", "tensor"),
        P("expert", "tensor", "dp"),
        P(("dp", "tensor"), None),
    )
    return jax.shard_map(
        local,
        mesh=mesh,
        in_specs=placed,
        out_specs=(
            P(("dp", "tensor"), None),
            P(("dp", "tensor"), None),
            P(("dp", "tensor")),
            P(("dp", "tensor"), "expert"),
            P(("dp", "tensor"), "expert"),
            P(("dp", "tensor"), "expert"),
            P("expert", ("dp", "tensor")),
            P(("dp", "tensor")),
            P(("dp", "tensor"), None),
            P("expert", "dp", "tensor"),
            P("expert", "dp", "tensor"),
            P("expert", "tensor", "dp"),
        ),
        check_vma=False,
    )
```

profile of v0, /device:TPU:0, one launch (start us, length us, event | category | flops | bytes accessed | tf_op | source)
XLA Modules:
  0.0 2066.3 jit_solution(10520688691983808503)
XLA Ops:
  32.7 73.9 %collective-permute-done.7 = bf16[2,512,1536]{2,1,0:T(8,128)(2,1)} collective-permute-done((bf16[2,512,1536]{2,1,0:T(8,128)(2,1)}, bf16[2,512,1536]{2,1,0:T(8,128)(2,1)}, u32[]{:S(2)}, u32[]{:S(2)}) %collective-permute-start.7) | collective-permute-done | bytes 3145760 | tf_op jit(solution)/shard_map/ppermute | solution.py:30
  113.9 121.8 %collective-permute-done.1 = bf16[2,512,1536]{2,1,0:T(8,128)(2,1)} collective-permute-done((bf16[2,512,1536]{2,1,0:T(8,128)(2,1)}, bf16[2,512,1536]{2,1,0:T(8,128)(2,1)}, u32[]{:S(2)}, u32[]{:S(2)}) %collective-permute-start.1) | collective-permute-done | bytes 3145760 | tf_op jit(solution)/shard_map/ppermute | solution.py:30
  239.4 85.9 %all-reduce.13 = (bf16[1536]{0:T(1024)(128)(2,1)S(1)}, bf16[1536]{0:T(1024)(128)(2,1)}) all-reduce(bf16[1536]{0:T(1024)(128)(2,1)S(1)} %dynamic-update-slice, bf16[1536]{0:T(1024)(128)(2,1)S(1)} %dynamic-update-slice.1), channel_id=1, replica_groups=mesh['dp'=4,'expert'=4,'tensor'=2] {'dp','tensor'}, use_global_device_ids=true, to_apply=%add.8 | all-reduce | flops 3072 | bytes 12288
  327.1 88.1 %all_gather.43 = bf16[1536,128]{1,0:T(8,128)(2,1)S(1)} all-gather(bf16[192,128]{1,0:T(8,128)(2,1)S(1)} %copy-done.125), channel_id=1, replica_groups=mesh['dp'=4,'expert'=4,'tensor'=2] {'dp','tensor'}, dimensions={0}, use_global_device_ids=true | all-gather | bytes 442368 | tf_op jit(solution)/shard_map/all_gather | solution.py:121
  415.2 14.7 all_gather.44
  523.8 25.0 %all-reduce.26.cloned.1.call-done = (bf16[512,1536]{1,0:T(8,128)(2,1)}, bf16[512,1536]{1,0:T(8,128)(2,1)}) async-done(((bf16[512,1536]{1,0:T(8,128)(2,1)}, bf16[512,1536]{1,0:T(8,128)(2,1)}), (bf16[512,1536]{1,0:T(8,128)(2,1)}, bf16[512,1536]{1,0:T(8,128)(2,1)})) %all-reduce.26.cloned.1.call-update) | async-done | bytes 3145744 | tf_op jit(solution)/shard_map/psum | solution.py:208
  561.7 15.9 all-gather
  644.1 62.8 %all-gather.19.cloned.1.call-done = bf16[4,1536,512]{2,1,0:T(8,128)(2,1)} async-done(((bf16[4,384,512]{2,1,0:T(8,128)(2,1)}), bf16[4,1536,512]{2,1,0:T(8,128)(2,1)}) %all-gather.19.cloned.1.call-update) | async-done | bytes 6291472 | tf_op jit(solution)/shard_map/all_gather | solution.py:128
  712.1 110.0 %all-gather.21.cloned.1.call-done = bf16[4,512,1536]{2,1,0:T(8,128)(2,1)} async-done(((bf16[4,512,384]{2,1,0:T(8,128)(2,1)}), bf16[4,512,1536]{2,1,0:T(8,128)(2,1)}) %all-gather.21.cloned.1.call-update) | async-done | bytes 6291472 | tf_op jit(solution)/shard_map/all_gather | solution.py:129
  918.4 11.6 reduce_sum.293
  945.7 11.6 reduce_sum.280
  958.2 16.2 multiply_reduce_fusion.1
  990.9 16.6 multiply_reduce_fusion.3
  1020.9 25.4 %all-reduce.24.cloned.1.call-done = (bf16[512,1536]{1,0:T(8,128)(2,1)}, bf16[512,1536]{1,0:T(8,128)(2,1)}) async-done(((bf16[512,1536]{1,0:T(8,128)(2,1)}, bf16[512,1536]{1,0:T(8,128)(2,1)}), (bf16[512,1536]{1,0:T(8,128)(2,1)}, bf16[512,1536]{1,0:T(8,128)(2,1)})) %all-reduce.24.cloned.1.call-update) | async-done | bytes 3145744 | tf_op jit(solution)/shard_map/psum | solution.py:288
  1120.9 11.4 copy.182
  1161.3 76.6 %all-reduce.22.cloned.1.call-done = (bf16[512,1536]{1,0:T(8,128)(2,1)}, bf16[512,1536]{1,0:T(8,128)(2,1)}, bf16[512,1536]{1,0:T(8,128)(2,1)}, bf16[512,1536]{1,0:T(8,128)(2,1)}) async-done(((bf16[512,1536]{1,0:T(8,128)(2,1)}, bf16[512,1536]{1,0:T(8,128)(2,1)}, bf16[512,1536]{1,0:T(8,128)(2,1)}, bf16[512,1536]{1,0:T(8,128)(2,1)}), (bf16[512,1536]{1,0:T(8,128)(2,1)}, bf16[512,1536]{1,0:T(8,128)(2,1)}, ...) | async-done | bytes 6291472 | tf_op jit(solution)/shard_map/psum | solution.py:355
  1273.8 149.5 %collective-permute-done.10 = bf16[2,512,1536]{2,1,0:T(8,128)(2,1)} collective-permute-done((bf16[2,512,1536]{2,1,0:T(8,128)(2,1)}, bf16[2,512,1536]{2,1,0:T(8,128)(2,1)}, u32[]{:S(2)}, u32[]{:S(2)}) %collective-permute-start.10) | collective-permute-done | bytes 3145760 | tf_op jit(solution)/shard_map/ppermute | solution.py:30
  1427.5 228.5 %collective-permute-done.4 = bf16[2,512,1536]{2,1,0:T(8,128)(2,1)} collective-permute-done((bf16[2,512,1536]{2,1,0:T(8,128)(2,1)}, bf16[2,512,1536]{2,1,0:T(8,128)(2,1)}, u32[]{:S(2)}, u32[]{:S(2)}) %collective-permute-start.4) | collective-permute-done | bytes 3145760 | tf_op jit(solution)/shard_map/ppermute | solution.py:30
  1673.7 15.5 reduce-scatter.33.cloned.1.call-done
  1692.7 223.6 %reduce-scatter.35.cloned.1.call-done = bf16[4,384,512]{2,1,0:T(8,128)(2,1)} async-done(((bf16[4,1536,512]{2,1,0:T(8,128)(2,1)}), bf16[4,384,512]{2,1,0:T(8,128)(2,1)}) %reduce-scatter.35.cloned.1.call-update) | async-done | bytes 1572880 | tf_op jit(solution)/shard_map/reduce_scatter | solution.py:392
  1919.8 28.7 %all-reduce.12 = (f32[1536]{0:T(1024)S(1)}, f32[1536]{0:T(1024)S(1)}) all-reduce(f32[1536]{0:T(1024)S(1)} %add.381, f32[1536]{0:T(1024)S(1)} %add.386), channel_id=6, replica_groups=mesh['dp'=4,'expert'=4,'tensor'=2] {'dp','tensor'}, use_global_device_ids=true, to_apply=%region_54.56.clone | all-reduce | flops 3072 | bytes 24576
  1958.4 24.4 %reduce-scatter.29.cloned.1.call-done = f32[192,128]{1,0:T(8,128)} async-done(((f32[1536,128]{1,0:T(8,128)}), f32[192,128]{1,0:T(8,128)}) %reduce-scatter.29.cloned.1.call-update) | async-done | bytes 98320 | tf_op jit(solution)/shard_map/reduce_scatter | solution.py:383
  1982.8 37.4 %reduce-scatter.25.cloned.1.call-done = f32[192,384]{1,0:T(8,128)} async-done(((f32[1536,384]{1,0:T(8,128)}), f32[192,384]{1,0:T(8,128)}) %reduce-scatter.25.cloned.1.call-update) | async-done | bytes 294928 | tf_op jit(solution)/shard_map/reduce_scatter | solution.py:381
  2020.2 38.6 %reduce-scatter.31.cloned.1.call-done = f32[384,192]{0,1:T(8,128)} async-done(((f32[384,1536]{0,1:T(8,128)}), f32[384,192]{0,1:T(8,128)}) %reduce-scatter.31.cloned.1.call-update) | async-done | bytes 294928 | tf_op jit(solution)/shard_map/reduce_scatter | solution.py:384
  (684 shorter events, 528.0 us)
Async XLA Ops:
  8.0 434.2 %all-gather.11.cloned.1.call-start = ((), (), s32[]{:S(2)}) async-start(), calls=%async_computation.12 | async-start | bytes 1327104 | tf_op jit(solution)/shard_map/all_gather | solution.py:119
  32.6 203.0 %collective-permute-start.1 = (bf16[2,512,1536]{2,1,0:T(8,128)(2,1)}, bf16[2,512,1536]{2,1,0:T(8,128)(2,1)}, u32[]{:S(2)}, u32[]{:S(2)}) collective-permute-start(bf16[2,512,1536]{2,1,0:T(8,128)(2,1)} %broadcast_select_fusion.7), channel_id=1, source_target_pairs={{0,8},{8,0},{1,9},{9,1},{16,24},{24,16},{17,25},{25,17},{2,10},{10... | collective-permute-start | bytes 9437192 | tf_op jit(solution)/shard_map/ppermute | solution.py:30
  32.7 423.7 %all-gather.13.cloned.1.call-start = ((), (), s32[]{:S(2)}) async-start(), calls=%async_computation.13 | async-start | bytes 1327104 | tf_op jit(solution)/shard_map/all_gather | solution.py:122
  110.7 320.1 %collective-permute-start.8 = (bf16[2,512,1536]{2,1,0:T(8,128)(2,1)}, bf16[2,512,1536]{2,1,0:T(8,128)(2,1)}, u32[]{:S(2)}, u32[]{:S(2)}) collective-permute-start(bf16[2,512,1536]{2,1,0:T(8,128)(2,1)} %broadcast_select_fusion.3), channel_id=1, source_target_pairs={{0,16},{16,0},{1,17},{17,1},{8,24},{24,8},{9,25},{25,9},{2,18},{18... | collective-permute-start | bytes 9437192 | tf_op jit(solution)/shard_map/ppermute | solution.py:30
  237.5 199.8 %collective-permute-start.2 = (bf16[2,512,1536]{2,1,0:T(8,128)(2,1)}, bf16[2,512,1536]{2,1,0:T(8,128)(2,1)}, u32[]{:S(2)}, u32[]{:S(2)}) collective-permute-start(bf16[2,512,1536]{2,1,0:T(8,128)(2,1)} %broadcast_select_fusion.9), channel_id=1, source_target_pairs={{0,16},{16,0},{1,17},{17,1},{8,24},{24,8},{9,25},{25,9},{2,18},{18... | collective-permute-start | bytes 9437192 | tf_op jit(solution)/shard_map/ppermute | solution.py:30
  237.5 311.3 %all-reduce.26.cloned.1.call-start = ((), (), s32[]{:S(2)}) async-start(), calls=%async_computation.35 | async-start | bytes 6291456 | tf_op jit(solution)/shard_map/psum | solution.py:208
  462.2 176.1 %all-gather.17.cloned.1.call-start = ((), (), s32[]{:S(2)}) async-start(), calls=%async_computation.15 | async-start | bytes 7864320 | tf_op jit(solution)/shard_map/all_gather | solution.py:127
  560.9 261.1 %all-gather.21.cloned.1.call-start = ((), (), s32[]{:S(2)}) async-start(), calls=%async_computation.17 | async-start | bytes 7864320 | tf_op jit(solution)/shard_map/all_gather | solution.py:129
  561.7 270.5 %all-gather.27.cloned.1.call-start = ((), (), s32[]{:S(2)}) async-start(), calls=%async_computation.23 | async-start | bytes 2949120 | tf_op jit(solution)/shard_map/all_gather | solution.py:255
  605.1 246.4 %all-gather.15.cloned.1.call-start = ((), (), s32[]{:S(2)}) async-start(), calls=%async_computation.14 | async-start | bytes 2949120 | tf_op jit(solution)/shard_map/all_gather | solution.py:219
  617.3 243.3 %all-gather.23.cloned.1.call-start = ((), (), s32[]{:S(2)}) async-start(), calls=%async_computation.19 | async-start | bytes 2949120 | tf_op jit(solution)/shard_map/all_gather | solution.py:255
  638.2 248.5 %reduce-scatter.21.cloned.1.call-start = ((), (), s32[]{:S(2)}) async-start(), calls=%async_computation.22 | async-start | bytes 2949120 | tf_op jit(solution)/shard_map/reduce_scatter | solution.py:229
  957.3 280.6 %all-reduce.22.cloned.1.call-start = ((), (), s32[]{:S(2)}) async-start(), calls=%async_computation.33 | async-start | bytes 12582912 | tf_op jit(solution)/shard_map/psum | solution.py:355
  1098.2 567.6 %reduce-scatter.37.cloned.1.call-start = ((), (), s32[]{:S(2)}) async-start(), calls=%async_computation.31 | async-start | bytes 884736
  1110.6 556.8 %reduce-scatter.39.cloned.1.call-start = ((), (), s32[]{:S(2)}) async-start(), calls=%async_computation.32 | async-start | bytes 7864320
  1140.5 548.7 %reduce-scatter.33.cloned.1.call-start = ((), (), s32[]{:S(2)}) async-start(), calls=%async_computation.29 | async-start | bytes 7864320 | tf_op jit(solution)/shard_map/reduce_scatter | solution.py:389
  1150.8 765.4 %reduce-scatter.35.cloned.1.call-start = ((), (), s32[]{:S(2)}) async-start(), calls=%async_computation.30 | async-start | bytes 7864320 | tf_op jit(solution)/shard_map/reduce_scatter | solution.py:392
  1160.8 797.6 %reduce-scatter.27.cloned.1.call-start = ((), (), s32[]{:S(2)}) async-start(), calls=%async_computation.26 | async-start | bytes 884736 | tf_op jit(solution)/shard_map/reduce_scatter | solution.py:382
  1256.2 726.6 %reduce-scatter.29.cloned.1.call-start = ((), (), s32[]{:S(2)}) async-start(), calls=%async_computation.27 | async-start | bytes 884736 | tf_op jit(solution)/shard_map/reduce_scatter | solution.py:383
  1260.2 760.0 %reduce-scatter.25.cloned.1.call-start = ((), (), s32[]{:S(2)}) async-start(), calls=%async_computation.25 | async-start | bytes 2654208 | tf_op jit(solution)/shard_map/reduce_scatter | solution.py:381
  1270.2 385.8 %collective-permute-start.4 = (bf16[2,512,1536]{2,1,0:T(8,128)(2,1)}, bf16[2,512,1536]{2,1,0:T(8,128)(2,1)}, u32[]{:S(2)}, u32[]{:S(2)}) collective-permute-start(bf16[2,512,1536]{2,1,0:T(8,128)(2,1)} %broadcast_select_fusion.6), channel_id=1, source_target_pairs={{0,8},{8,0},{1,9},{9,1},{16,24},{24,16},{17,25},{25,17},{2,10},{10... | collective-permute-start | bytes 9437192 | tf_op jit(solution)/shard_map/ppermute | solution.py:30
  1273.6 785.3 %reduce-scatter.31.cloned.1.call-start = ((), (), s32[]{:S(2)}) async-start(), calls=%async_computation.28 | async-start | bytes 2654208 | tf_op jit(solution)/shard_map/reduce_scatter | solution.py:384
  1427.4 522.4 %collective-permute-start.11 = (bf16[2,512,1536]{2,1,0:T(8,128)(2,1)}, bf16[2,512,1536]{2,1,0:T(8,128)(2,1)}, u32[]{:S(2)}, u32[]{:S(2)}) collective-permute-start(bf16[2,512,1536]{2,1,0:T(8,128)(2,1)} %broadcast_select_fusion.2), channel_id=1, source_target_pairs={{0,16},{16,0},{1,17},{17,1},{8,24},{24,8},{9,25},{25,9},{2,18},{18... | collective-permute-start | bytes 9437192 | tf_op jit(solution)/shard_map/ppermute | solution.py:30
  1657.9 294.3 %collective-permute-start.5 = (bf16[2,512,1536]{2,1,0:T(8,128)(2,1)}, bf16[2,512,1536]{2,1,0:T(8,128)(2,1)}, u32[]{:S(2)}, u32[]{:S(2)}) collective-permute-start(bf16[2,512,1536]{2,1,0:T(8,128)(2,1)} %broadcast_select_fusion.8), channel_id=1, source_target_pairs={{0,16},{16,0},{1,17},{17,1},{8,24},{24,8},{9,25},{25,9},{2,18},{18... | collective-permute-start | bytes 9437192 | tf_op jit(solution)/shard_map/ppermute | solution.py:30
  (179 other events, 5456.7 us)
Sparse Core Ops, SparseCore 0:
  32.8 30.5 all-gather.10
  237.6 89.1 all-gather.12
  462.3 86.4 all-reduce.25
  957.4 88.8 all-reduce.23
  1098.3 139.5 all-reduce.21
  1240.0 35.6 reduce-scatter.36
  1278.2 207.0 reduce-scatter.38
  1487.7 201.4 reduce-scatter.32
  1691.6 224.6 reduce-scatter.34
  1919.1 31.1 reduce-scatter.26
  1953.2 29.5 reduce-scatter.28
  1985.7 34.4 reduce-scatter.24
  2023.2 35.5 reduce-scatter.30
Sparse Core Ops, SparseCore 1:
  464.3 114.7 all-gather.16
  580.5 8.5 all-gather.24
  590.6 116.3 all-gather.18
  708.6 113.3 all-gather.20
  823.7 8.5 all-gather.26
  833.8 11.4 all-gather.14
  846.8 11.5 all-gather.22
  861.1 10.6 reduce-scatter.20
  873.9 10.6 reduce-scatter.22
  886.9 10.5 reduce-scatter.18
  899.6 10.6 reduce-scatter.16
where the time goes:
time: 2070 us
  waiting for transfers between devices  1230 us (59%)
  blocking collectives  244 us (12%)
  local copies, waits for them, and re-layouts  197 us (10%)
  other arithmetic  186 us (9%)
  matrix products  174 us (8%)
  between operations  24.9 us (1%)
    ppermute x12, waiting for transfers between devices, partner_2(): return lax.ppermute(block, axis, route)  574 us
    reduce_scatter x1, waiting for transfers between devices, local(): lax.psum_scatter(expert_sums[1].astype(jnp.bfloat16), 'dp', scatter_dimen...  224 us
    unnamed x2, blocking collectives  115 us
    all_gather x1, waiting for transfers between devices, local(): lax.all_gather(w_down, 'dp', axis=2, tiled=True)  110 us
    all_gather x1, blocking collectives, local(): lax.all_gather(w_value, ('dp', 'tensor'), axis=0, tiled=True)  88.1 us
    psum x1, waiting for transfers between devices, local(): lax.psum(norm_part.astype(jnp.bfloat16), 'expert').astype(jnp.float32)  76.6 us
    all_gather x1, waiting for transfers between devices, local(): lax.all_gather(w_up, 'dp', axis=1, tiled=True)  62.8 us
    unnamed x350, local copies, waits for them, and re-layouts  47.4 us
  transfers between devices with their start and end apart: 36, of which 16 were waited for; matrix products, arithmetic and copies ran while one was open for 23% of the time, Pallas kernels for 0%

commit v1 on v0

v1 whole, which is shorter than its diff:
```python
import math

import jax
import jax.numpy as jnp
from jax import lax
from jax.experimental import pallas as pl
from jax.experimental.pallas import tpu as pltpu
from jax.sharding import PartitionSpec as P

D = 1536
HEADS = 24
KV_HEADS = 8
HEAD_DIM = 64
EXPERTS = 16
FF = 1024
TOP = 2
SEQ_LEN = 512
MICRO = 2
CAP = 80

BF = jnp.bfloat16
F32 = jnp.float32
norm_epsilon = 1e-05
masked_score = -1e30
score_scale = 1.0 / math.sqrt(HEAD_DIM)
HALF = SEQ_LEN // 2


def matmul(left, right):
    return lax.dot_general(left, right, (((1,), (0,)), ((), ())), preferred_element_type=F32)


def matmul_nt(left, right):
    return lax.dot_general(left, right, (((1,), (1,)), ((), ())), preferred_element_type=F32)


def matmul_tn(left, right):
    return lax.dot_general(left, right, (((0,), (0,)), ((), ())), preferred_element_type=F32)


def rms_scale(values):
    return lax.rsqrt(jnp.mean(values * values, axis=-1, keepdims=True) + norm_epsilon)


def swap(block, axis, distance):
    count = lax.axis_size(axis)
    return lax.ppermute(block, axis, [(low, low ^ distance) for low in range(count)])


def pick(stacked, index):
    return lax.dynamic_index_in_dim(stacked, index, 0, keepdims=False)


def attention_forward_kernel(length_ref, qkv_ref, mixed_ref, probs_low_ref, probs_high_ref):
    heads = probs_low_ref.shape[0]
    kv_heads = heads * KV_HEADS // HEADS
    groups = heads // kv_heads
    length_one = length_ref[0]
    key_base = heads * HEAD_DIM
    value_base = key_base + kv_heads * HEAD_DIM
    value_t = qkv_ref[:, value_base : value_base + kv_heads * HEAD_DIM].astype(F32).T.astype(BF)
    key_at = lax.broadcasted_iota(jnp.int32, (HALF, HALF), 0)
    query_at = lax.broadcasted_iota(jnp.int32, (HALF, HALF), 1)
    causal = key_at <= query_at
    ragged = causal & (key_at + HALF < length_one)
    for kv in range(kv_heads):
        keys = qkv_ref[:, key_base + kv * HEAD_DIM : key_base + (kv + 1) * HEAD_DIM]
        values = value_t[kv * HEAD_DIM : (kv + 1) * HEAD_DIM, :]
        for group in range(groups):
            head = kv * groups + group
            lanes = slice(head * HEAD_DIM, (head + 1) * HEAD_DIM)
            query = qkv_ref[:, lanes] * jnp.asarray(score_scale, BF)
            first = jnp.where(causal, matmul_nt(keys[:HALF], query[:HALF]), masked_score)
            first = jnp.exp(first - jnp.max(first, axis=0, keepdims=True))
            first = (first * (1.0 / jnp.sum(first, axis=0, keepdims=True))).astype(BF)
            probs_low_ref[head] = first
            upper = matmul_nt(keys[:HALF], query[HALF:])
            lower = jnp.where(ragged, matmul_nt(keys[HALF:], query[HALF:]), masked_score)
            highest = jnp.maximum(
                jnp.max(upper, axis=0, keepdims=True), jnp.max(lower, axis=0, keepdims=True)
            )
            upper = jnp.exp(upper - highest)
            lower = jnp.exp(lower - highest)
            inverse = 1.0 / (
                jnp.sum(upper, axis=0, keepdims=True) + jnp.sum(lower, axis=0, keepdims=True)
            )
            upper = (upper * inverse).astype(BF)
            lower = (lower * inverse).astype(BF)
            probs_high_ref[head, :HALF] = upper
            probs_high_ref[head, HALF:] = lower
            left = matmul(values[:, :HALF], first)
            right = matmul(values[:, :HALF], upper) + matmul(values[:, HALF:], lower)
            mixed_ref[:HALF, lanes] = left.T.astype(BF)
            mixed_ref[HALF:, lanes] = right.T.astype(BF)


def attention_forward(length_one, qkv):
    heads = qkv.shape[1] * HEADS // ((HEADS + 2 * KV_HEADS) * HEAD_DIM)
    vmem = pl.BlockSpec(memory_space=pltpu.VMEM)
    return pl.pallas_call(
        attention_forward_kernel,
        in_specs=[pl.BlockSpec(memory_space=pltpu.SMEM), vmem],
        out_specs=[vmem, vmem, vmem],
        out_shape=[
            jax.ShapeDtypeStruct((SEQ_LEN, heads * HEAD_DIM), BF),
            jax.ShapeDtypeStruct((heads, HALF, HALF), BF),
            jax.ShapeDtypeStruct((heads, SEQ_LEN, HALF), BF),
        ],
        compiler_params=pltpu.CompilerParams(vmem_limit_bytes=32 << 20),
        name="attention_forward",
    )(length_one.reshape(1), qkv)


def attention_backward_kernel(
    qkv_ref, mixed_ref, grad_ref, probs_low_ref, probs_high_ref, grad_qkv_ref
):
    heads = probs_low_ref.shape[0]
    kv_heads = heads * KV_HEADS // HEADS
    groups = heads // kv_heads
    key_base = heads * HEAD_DIM
    value_base = key_base + kv_heads * HEAD_DIM
    product_t = (mixed_ref[...].astype(F32) * grad_ref[...].astype(F32)).T
    key_t = qkv_ref[:, key_base : key_base + kv_heads * HEAD_DIM].astype(F32).T.astype(BF)
    for kv in range(kv_heads):
        keys = slice(key_base + kv * HEAD_DIM, key_base + (kv + 1) * HEAD_DIM)
        values = slice(value_base + kv * HEAD_DIM, value_base + (kv + 1) * HEAD_DIM)
        value_rows = qkv_ref[:, values]
        keys_t = key_t[kv * HEAD_DIM : (kv + 1) * HEAD_DIM, :]
        grad_key_top = grad_key_bottom = grad_value_top = grad_value_bottom = 0.0
        for group in range(groups):
            head = kv * groups + group
            lanes = slice(head * HEAD_DIM, (head + 1) * HEAD_DIM)
            inner = jnp.sum(product_t[lanes, :], axis=0, keepdims=True)
            query = qkv_ref[:, lanes] * jnp.asarray(score_scale, BF)
            grad = grad_ref[:, lanes]
            first = probs_low_ref[head]
            upper = probs_high_ref[head, :HALF]
            lower = probs_high_ref[head, HALF:]
            grad_first = matmul_nt(value_rows[:HALF], grad[:HALF]) - inner[:, :HALF]
            grad_upper = matmul_nt(value_rows[:HALF], grad[HALF:]) - inner[:, HALF:]
            grad_lower = matmul_nt(value_rows[HALF:], grad[HALF:]) - inner[:, HALF:]
            grad_first = (first.astype(F32) * grad_first).astype(BF)
            grad_upper = (upper.astype(F32) * grad_upper).astype(BF)
            grad_lower = (lower.astype(F32) * grad_lower).astype(BF)
            left = matmul(keys_t[:, :HALF], grad_first)
            right = matmul(keys_t[:, :HALF], grad_upper) + matmul(keys_t[:, HALF:], grad_lower)
            grad_qkv_ref[:HALF, lanes] = (left * score_scale).T.astype(BF)
            grad_qkv_ref[HALF:, lanes] = (right * score_scale).T.astype(BF)
            grad_key_top += matmul(grad_first, query[:HALF]) + matmul(grad_upper, query[HALF:])
            grad_key_bottom += matmul(grad_lower, query[HALF:])
            grad_value_top += matmul(first, grad[:HALF]) + matmul(upper, grad[HALF:])
            grad_value_bottom += matmul(lower, grad[HALF:])
        grad_qkv_ref[:HALF, keys] = grad_key_top.astype(BF)
        grad_qkv_ref[HALF:, keys] = grad_key_bottom.astype(BF)
        grad_qkv_ref[:HALF, values] = grad_value_top.astype(BF)
        grad_qkv_ref[HALF:, values] = grad_value_bottom.astype(BF)


def attention_backward(qkv, mixed, grad_mixed, probs_low, probs_high):
    vmem = pl.BlockSpec(memory_space=pltpu.VMEM)
    return pl.pallas_call(
        attention_backward_kernel,
        in_specs=[vmem] * 5,
        out_specs=vmem,
        out_shape=jax.ShapeDtypeStruct(qkv.shape, BF),
        compiler_params=pltpu.CompilerParams(vmem_limit_bytes=32 << 20),
        name="attention_backward",
    )(qkv, mixed, grad_mixed, probs_low, probs_high)


def local(
    tokens,
    deal,
    lengths,
    priority,
    routes,
    gain_attn,
    w_query,
    w_key,
    w_value,
    w_out,
    gain_ffn,
    w_router,
    w_gate,
    w_up,
    w_down,
    cotangent,
):
    owners = ("dp", "tensor")
    n_dp = lax.axis_size("dp")
    n_tensor = lax.axis_size("tensor")
    n_expert = lax.axis_size("expert")
    n_owner = n_dp * n_tensor
    local_experts = EXPERTS // n_expert
    outer = n_dp // local_experts
    assert n_tensor == 2 and outer * local_experts == n_dp
    dp_index = lax.axis_index("dp")
    tensor_index = lax.axis_index("tensor")
    expert_index = lax.axis_index("expert")
    inner_index = dp_index % local_experts
    inner_groups = [
        [group * local_experts + at for at in range(local_experts)] for group in range(outer)
    ]
    outer_groups = [
        [group * local_experts + at for group in range(outer)] for at in range(local_experts)
    ]
    rows_own = SEQ_LEN // n_expert
    width = D // n_owner
    chunk = D // n_dp
    head_lanes = HEADS // n_expert * HEAD_DIM
    kv_lanes = KV_HEADS // n_expert * HEAD_DIM
    lower_core = tensor_index == 0

    def across_inner(block):
        if outer == 1:
            return lax.all_to_all(block, "dp", 0, 0, tiled=True)
        return lax.all_to_all(block, "dp", 0, 0, tiled=True, axis_index_groups=inner_groups)

    def gather_dp(block):
        spread = jnp.broadcast_to(block[None], (n_dp,) + block.shape)
        return lax.all_to_all(spread, "dp", 0, 0, tiled=True)

    def both_cores(block, axis):
        other = swap(block, "tensor", 1)
        low = jnp.where(lower_core, block, other)
        high = jnp.where(lower_core, other, block)
        return jnp.stack([low, high], axis=axis)

    routes_t = routes.T.reshape(TOP, MICRO, SEQ_LEN)
    table = jnp.stack(
        [
            priority.reshape(MICRO, SEQ_LEN),
            routes_t[0],
            routes_t[1],
            jnp.broadcast_to(lengths[:, None], (MICRO, SEQ_LEN)),
        ],
        axis=1,
    )
    tables = lax.all_gather(table, owners, axis=0, tiled=True)
    small = jnp.concatenate([w_router.T, gain_attn[None], gain_ffn[None]], axis=0)
    smalls = lax.all_gather(small, owners, axis=0)
    smalls = smalls.transpose(1, 0, 2).reshape(EXPERTS + 2, D)
    router_t = smalls[:EXPERTS]
    gain_one = smalls[EXPERTS].astype(F32)[None]
    gain_two = smalls[EXPERTS + 1].astype(F32)[None]

    w_qkv = gather_dp(jnp.concatenate([w_query, w_key, w_value], axis=1))
    w_qkv = both_cores(w_qkv, 1).reshape(D, head_lanes + 2 * kv_lanes)

    normed_one = []
    qkv_rows = []
    mixed_rows = []
    probs_kept = []
    sequence_tables = []
    for micro in range(MICRO):
        rows = slice(micro * SEQ_LEN, (micro + 1) * SEQ_LEN)
        inputs = tokens[rows].astype(F32)
        normed = (inputs * rms_scale(inputs) * gain_one).astype(BF)
        qkv = matmul(normed, w_qkv).astype(BF)
        own_table = pick(tables, deal[micro])
        mixed, probs_low, probs_high = attention_forward(own_table[3, 0], qkv)
        normed_one.append(normed)
        qkv_rows.append(qkv)
        mixed_rows.append(mixed)
        probs_kept.append((probs_low, probs_high))
        sequence_tables.append(own_table)

    w_out_part = gather_dp(w_out.T)
    w_out_parts = [w_out_part] + [swap(w_out_part, "expert", far) for far in range(1, n_expert)]
    w_out_t = both_cores(jnp.concatenate(w_out_parts, axis=2), 1)
    w_out_t = w_out_t.reshape(D, n_expert * head_lanes)

    def collect(weight):
        if outer > 1:
            weight = lax.all_gather(weight, "dp", axis=0, axis_index_groups=outer_groups)
            weight = across_inner(jnp.swapaxes(weight, 0, 1))
            weight = jnp.swapaxes(weight, 0, 1)
            return weight.reshape((n_dp,) + weight.shape[2:])
        return across_inner(weight)

    def with_other(weight, axis):
        return jnp.concatenate([weight, swap(weight, "tensor", 1)], axis=axis)

    half_ff = w_gate.shape[2]
    gate_weight = with_other(collect(w_gate).reshape(D, half_ff), 1)
    up_weight = with_other(collect(w_up).reshape(D, half_ff), 1)
    down_weight = with_other(collect(w_down).transpose(1, 0, 2).reshape(half_ff, D), 0)

    positions = jnp.arange(SEQ_LEN, dtype=jnp.int32)
    expert_ids = expert_index * local_experts + jnp.bitwise_xor(
        inner_index, jnp.arange(local_experts, dtype=jnp.int32)
    )
    places = jnp.arange(CAP, dtype=F32)[None, :, None]

    def nearest_first(lanes):
        blocks = lanes.reshape(local_experts, n_expert, rows_own)
        return jnp.concatenate(
            [
                lax.dynamic_index_in_dim(blocks, expert_index ^ far, 1, keepdims=False)
                for far in range(n_expert)
            ],
            axis=1,
        )

    def selections(own_table):
        rank, first, second, live_count = own_table
        live = positions < live_count
        wanted = expert_ids[:, None]
        chosen = ((first[None] == wanted) | (second[None] == wanted)) & live[None]
        chosen = chosen.astype(BF)
        earlier = (rank[:, None] < rank[None, :]).astype(BF)
        place = matmul(chosen, earlier)
        place = jnp.where(chosen > 0, place, -1.0)
        given = (place[:, None, :] == places).astype(BF)
        near = (nearest_first(place)[:, None, :] == places).astype(BF)
        return given, near

    def to_experts(given, rows):
        blocks = [matmul(given[far], rows).astype(BF) for far in range(local_experts)]
        return jnp.concatenate(
            [blocks[0]] + [swap(blocks[far], "dp", far) for far in range(1, local_experts)], axis=0
        )

    def from_experts(near, slots):
        blocks = [slots[far * CAP : (far + 1) * CAP] for far in range(local_experts)]
        slots = jnp.concatenate(
            [blocks[0]] + [swap(blocks[far], "dp", far) for far in range(1, local_experts)], axis=0
        )
        near = near.reshape(local_experts * CAP, n_expert, rows_own)
        parts = [matmul_tn(near[:, far], slots).astype(BF) for far in range(n_expert)]
        return sum_over_groups(parts)

    def sum_over_groups(parts):
        total = parts[0].astype(F32)
        for far in range(1, n_expert):
            total = total + swap(parts[far], "expert", far).astype(F32)
        return total

    def own_rows(array, micro):
        start = micro * SEQ_LEN + expert_index * rows_own
        return lax.dynamic_slice_in_dim(array, start, rows_own, 0)

    def spread_rows(blocks):
        whole = jnp.zeros((MICRO * SEQ_LEN, D), BF)
        for micro, block in enumerate(blocks):
            for far in range(n_expert):
                piece = swap(block, "expert", far) if far else block
                start = micro * SEQ_LEN + (expert_index ^ far) * rows_own
                whole = lax.dynamic_update_slice(whole, piece, (start, 0))
        return whole

    chosen_expert = expert_index * local_experts + inner_index
    expert_mask = (jnp.arange(EXPERTS, dtype=jnp.int32) == chosen_expert).astype(F32)[None]

    selected = [selections(sequence_tables[micro]) for micro in range(MICRO)]
    grad_slots = [
        to_experts(selected[micro][0], cotangent[micro * SEQ_LEN : (micro + 1) * SEQ_LEN])
        for micro in range(MICRO)
    ]

    mixed_own = []
    hidden_own = []
    scale_own = []
    slot_rows = []
    for micro in range(MICRO):
        pieces = mixed_rows[micro].reshape(n_expert, rows_own, head_lanes)
        mixed_all = jnp.concatenate(
            [pick(pieces, expert_index)]
            + [
                swap(pick(pieces, expert_index ^ far), "expert", far)
                for far in range(1, n_expert)
            ],
            axis=1,
        )
        hidden_one = own_rows(tokens, micro).astype(F32) + matmul_nt(mixed_all, w_out_t)
        scale_two = rms_scale(hidden_one)
        normed_two = (hidden_one * scale_two * gain_two).astype(BF)
        normed_all = jnp.concatenate(
            [normed_two] + [swap(normed_two, "expert", far) for far in range(1, n_expert)], axis=0
        )
        slot_rows.append(to_experts(selected[micro][1], normed_all))
        mixed_own.append(mixed_all)
        hidden_own.append(hidden_one)
        scale_own.append(scale_two)

    result_own = []
    grad_hidden_own = []
    grad_two_own = []
    hidden_scaled = []
    grads_gate = []
    grads_up = []
    router_grad = 0.0
    for micro in range(MICRO):
        slots = slot_rows[micro]
        cots = grad_slots[micro]
        logits = matmul_nt(slots, router_t)
        router = jax.nn.softmax(logits, axis=-1)
        gates = jnp.sum(router * expert_mask, axis=1, keepdims=True)
        gate_in = matmul(slots, gate_weight)
        up_in = matmul(slots, up_weight)
        cot_hidden = matmul_nt(cots, down_weight)
        sigmoid_in = jax.nn.sigmoid(gate_in)
        activated = gate_in * sigmoid_in
        hidden_float = activated * up_in
        hidden = hidden_float.astype(BF)
        grad_hidden = gates * cot_hidden
        grad_gate_in = (
            grad_hidden * up_in * (sigmoid_in * (1.0 + gate_in * (1.0 - sigmoid_in)))
        ).astype(BF)
        grad_up_in = (grad_hidden * activated).astype(BF)
        gate_grad = jnp.sum(hidden.astype(F32) * cot_hidden, axis=1, keepdims=True)
        grad_logits = (gate_grad * gates * (expert_mask - router)).astype(BF)
        grad_rows = (
            matmul_nt(grad_gate_in, gate_weight)
            + matmul_nt(grad_up_in, up_weight)
            + matmul(grad_logits, router_t)
        ).astype(BF)
        grad_two_own.append(from_experts(selected[micro][1], grad_rows))
        expert_out = (gates * matmul(hidden, down_weight)).astype(BF)
        expert_mix = from_experts(selected[micro][1], expert_out)
        result_own.append((hidden_own[micro] + expert_mix).astype(BF))
        router_grad = router_grad + matmul_tn(grad_logits, slots)
        hidden_scaled.append((gates * hidden_float).astype(BF))
        grads_gate.append(grad_gate_in)
        grads_up.append(grad_up_in)

    def over_micro(lefts, rights):
        return sum(matmul_tn(left, right) for left, right in zip(lefts, rights))

    def halves(blocks, at):
        return [block[:, at * half_ff : (at + 1) * half_ff] for block in blocks]

    def join_cores(own, other):
        return own + swap(other.astype(BF), "tensor", 1).astype(F32)

    def scatter_back(pieces):
        if outer > 1:
            pieces = pieces.reshape((outer, local_experts) + pieces.shape[1:])
            pieces = across_inner(jnp.swapaxes(pieces, 0, 1))
            pieces = jnp.swapaxes(pieces, 0, 1)
            pieces = lax.psum_scatter(
                pieces, "dp", scatter_dimension=0, axis_index_groups=outer_groups
            )
            return pieces.astype(F32)
        return across_inner(pieces).astype(F32)

    d_gate = join_cores(
        over_micro(slot_rows, halves(grads_gate, 0)), over_micro(slot_rows, halves(grads_gate, 1))
    )
    d_gate = scatter_back(d_gate.astype(BF).reshape(n_dp, chunk, half_ff))
    d_up = join_cores(
        over_micro(slot_rows, halves(grads_up, 0)), over_micro(slot_rows, halves(grads_up, 1))
    )
    d_up = scatter_back(d_up.astype(BF).reshape(n_dp, chunk, half_ff))
    d_down = join_cores(
        over_micro(halves(hidden_scaled, 0), grad_slots),
        over_micro(halves(hidden_scaled, 1), grad_slots),
    )
    d_down = d_down.astype(BF).reshape(half_ff, n_dp, chunk).transpose(1, 0, 2)
    d_down = scatter_back(d_down)

    grad_hidden_own = []
    gain_two_grad = 0.0
    branch_own = []
    grad_qkv_rows = []
    grad_one_own = []
    for micro in range(MICRO):
        grad_two = grad_two_own[micro]
        hidden_one = hidden_own[micro]
        scale_two = scale_own[micro]
        gain_two_grad = gain_two_grad + jnp.sum(grad_two * hidden_one * scale_two, axis=0)
        weighted = grad_two * gain_two
        inner = jnp.mean(hidden_one * weighted, axis=-1, keepdims=True)
        grad_hidden_one = (
            own_rows(cotangent, micro).astype(F32)
            + scale_two * weighted
            - hidden_one * (scale_two * scale_two * scale_two) * inner
        )
        grad_branch = grad_hidden_one.astype(BF)
        grad_mixed = matmul(grad_branch, w_out_t).astype(BF)
        pieces = [
            grad_mixed[:, far * head_lanes : (far + 1) * head_lanes] for far in range(n_expert)
        ]
        pieces = [pieces[0]] + [swap(pieces[far], "expert", far) for far in range(1, n_expert)]
        near = jnp.stack(pieces, axis=0)
        grad_heads = jnp.concatenate(
            [pick(near, expert_index ^ at) for at in range(n_expert)], axis=0
        )
        grad_qkv = attention_backward(
            qkv_rows[micro], mixed_rows[micro], grad_heads, *probs_kept[micro]
        )
        blocks = grad_qkv.reshape(n_expert, rows_own, grad_qkv.shape[1])
        parts = [
            matmul_nt(pick(blocks, expert_index ^ far), w_qkv).astype(BF) for far in range(n_expert)
        ]
        grad_one_own.append(sum_over_groups(parts))
        grad_hidden_own.append(grad_hidden_one)
        branch_own.append(grad_branch)
        grad_qkv_rows.append(grad_qkv)

    def split_cores(pieces, axis):
        own = lax.dynamic_index_in_dim(pieces, tensor_index, axis, keepdims=False)
        other = lax.dynamic_index_in_dim(pieces, 1 - tensor_index, axis, keepdims=False)
        return join_cores(own, other)

    def sum_dp(pieces):
        pieces = lax.all_to_all(pieces.astype(BF), "dp", 0, 0, tiled=True)
        return jnp.sum(pieces.astype(F32), axis=0)

    d_out = [
        over_micro(
            branch_own,
            [mixed[:, far * head_lanes : (far + 1) * head_lanes] for mixed in mixed_own],
        )
        .reshape(n_dp, n_tensor, width, head_lanes)
        for far in range(n_expert)
    ]
    d_out = [split_cores(part, 1).astype(BF) for part in d_out]
    d_out = sum_dp(sum_over_groups(d_out)).T

    d_qkv = over_micro(normed_one, grad_qkv_rows)
    d_qkv = split_cores(d_qkv.reshape(n_dp, n_tensor, width, d_qkv.shape[1]), 1)
    d_qkv = sum_dp(d_qkv)

    gain_one_grad = 0.0
    grad_inputs_own = []
    for micro in range(MICRO):
        grad_one = grad_one_own[micro]
        inputs = own_rows(tokens, micro).astype(F32)
        scale_one = rms_scale(inputs)
        gain_one_grad = gain_one_grad + jnp.sum(grad_one * inputs * scale_one, axis=0)
        weighted = grad_one * gain_one
        inner = jnp.mean(inputs * weighted, axis=-1, keepdims=True)
        grad_inputs = (
            grad_hidden_own[micro]
            + scale_one * weighted
            - inputs * (scale_one * scale_one * scale_one) * inner
        )
        grad_inputs_own.append(grad_inputs.astype(BF))

    everywhere = ("dp", "expert", "tensor")
    owner_index = lax.axis_index(owners)
    early = lax.psum(jnp.concatenate([router_grad, gain_two_grad[None]], axis=0), everywhere)
    early = lax.dynamic_slice_in_dim(early, owner_index * width, width, 1)
    late = lax.psum(gain_one_grad, everywhere)
    late = lax.dynamic_slice_in_dim(late, owner_index * width, width, 0)

    return (
        spread_rows(result_own),
        spread_rows(grad_inputs_own),
        late,
        d_qkv[:, :head_lanes],
        d_qkv[:, head_lanes : head_lanes + kv_lanes],
        d_qkv[:, head_lanes + kv_lanes :],
        d_out,
        early[EXPERTS],
        early[:EXPERTS].T,
        d_gate,
        d_up,
        d_down,
    )


def solution(mesh):
    placed = (
        P(("dp", "tensor"), None),
        P(("dp", "tensor")),
        P(("dp", "tensor")),
        P(("dp", "tensor")),
        P(("dp", "tensor"), None),
        P(("dp", "tensor")),
        P(("dp", "tensor"), "expert"),
        P(("dp", "tensor"), "expert"),
        P(("dp", "tensor"), "expert"),
        P("expert", ("dp", "tensor")),
        P(("dp", "tensor")),
        P(("dp", "tensor"), None),
        P("expert", "dp", "tensor"),
        P("expert", "dp", "tensor"),
        P("expert", "tensor", "dp"),
        P(("dp", "tensor"), None),
    )
    return jax.shard_map(
        local,
        mesh=mesh,
        in_specs=placed,
        out_specs=(
            P(("dp", "tensor"), None),
            P(("dp", "tensor"), None),
            P(("dp", "tensor")),
            P(("dp", "tensor"), "expert"),
            P(("dp", "tensor"), "expert"),
            P(("dp", "tensor"), "expert"),
            P("expert", ("dp", "tensor")),
            P(("dp", "tensor")),
            P(("dp", "tensor"), None),
            P("expert", "dp", "tensor"),
            P("expert", "dp", "tensor"),
            P("expert", "tensor", "dp"),
        ),
        check_vma=False,
    )
```

time: 2070 us -> 851 us (0.41)
  waiting for transfers between devices: 1230 us -> 299 us
  blocking collectives: 244 us -> 82.9 us
  starting transfers between devices: 15 us -> 161 us
  other arithmetic: 186 us -> 41.1 us
  local copies, waits for them, and re-layouts: 197 us -> 69.6 us
    ppermute x12 -> x91, waiting for transfers between devices: 574 us -> 172 us  [swap(): lax.ppermute(block, axis, [(low, low ^ distance) for low in range(count)])]
    reduce_scatter x10 -> x0, waiting for transfers between devices: 339 us -> none  [the longest x1 224 us: local(): lax.psum_scatter(expert_sums[1].astype(jnp.bfloat16), 'dp', scatter_dimen...]
    all_gather x9 -> x0, waiting for transfers between devices: 183 us -> none  [the longest x1 110 us: local(): lax.all_gather(w_down, 'dp', axis=2, tiled=True)]
    unnamed x2 -> x0, blocking collectives: 115 us -> none
    gather x26 -> x0, local copies, waits for them, and re-layouts: 110 us -> none  [the longest x4 28.9 us: local(): picked = flat_out[local_slot]]
    ppermute x12 -> x91, starting transfers between devices: 12.8 us -> 113 us  [swap(): lax.ppermute(block, axis, [(low, low ^ distance) for low in range(count)])]
    all_gather x3 -> x2, blocking collectives: 119 us -> 42.3 us  [the longest x1 23.2 us: local(): smalls = lax.all_gather(small, owners, axis=0)]
    reduce_sum x14 -> x3, other arithmetic: 67.9 us -> 2.27 us  [the longest x2 2.18 us: sum_dp(): return jnp.sum(pieces.astype(F32), axis=0)]
  transfers between devices with their start and end apart: 36 -> 102, of which waited for: 16 -> 30; matrix products, arithmetic and copies ran while one was open for 23% -> 29% of each run, Pallas kernels for 0% -> 2%
where the time goes in v1:
time: 851 us; the launch traced here: 843 us
  waiting for transfers between devices  299 us (35%)
  starting transfers between devices  161 us (19%)
  matrix products  156 us (18%)
  blocking collectives  82.9 us (10%)
  local copies, waits for them, and re-layouts  69.6 us (8%)
  other arithmetic  41.1 us (5%)
  between operations  20.2 us (2%)
  Pallas kernels  13.7 us (2%)
    ppermute x91, waiting for transfers between devices, swap(): lax.ppermute(block, axis, [(low, low ^ distance) for low in range(count)])  172 us
    ppermute x91, starting transfers between devices, swap(): lax.ppermute(block, axis, [(low, low ^ distance) for low in range(count)])  113 us
    psum x1, waiting for transfers between devices, local(): lax.psum(jnp.concatenate([router_grad, gain_two_grad[None]], axis=0), eve...  109 us
    dot_general x40, matrix products, matmul_tn(): lax.dot_general(left, right, (((0,), (0,)), ((), ())), preferred_element_...  62.2 us
    dot_general x30, matrix products, matmul(): lax.dot_general(left, right, (((1,), (0,)), ((), ())), preferred_element_...  54.2 us
    psum x1, blocking collectives, local(): late = lax.psum(gain_one_grad, everywhere)  40.6 us
    dot_general x18, matrix products, matmul_nt(): lax.dot_general(left, right, (((1,), (1,)), ((), ())), preferred_element_...  39.4 us
    all_to_all x6, starting transfers between devices, across_inner(): return lax.all_to_all(block, 'dp', 0, 0, tiled=True)  29.1 us
  transfers between devices with their start and end apart: 102, of which 30 were waited for; matrix products, arithmetic and copies ran while one was open for 29% of the time, Pallas kernels for 2%

profile of v1, /device:TPU:0, one launch (start us, length us, event | category | flops | bytes accessed | tf_op | source)
XLA Modules:
  0.0 842.8 jit_solution(10273369698335452854)
XLA Ops:
  9.2 6.3 all-to-all-start.1
  18.8 19.1 %all_gather.9 = s32[16,4,512]{2,1,0:T(4,128)S(1)} all-gather(s32[2,4,512]{2,1,0:T(4,128)S(1)} %pad_add_fusion), channel_id=1, replica_groups=mesh['dp'=4,'expert'=4,'tensor'=2] {'dp','tensor'}, dimensions={0}, use_global_device_ids=true | all-gather | bytes 147456 | tf_op jit(solution)/shard_map/all_gather | solution.py:239
  64.6 23.2 %all-gather.1 = bf16[8,18,192]{2,1,0:T(8,128)(2,1)S(1)} all-gather(bf16[1,18,192]{2,1,0:T(8,128)(2,1)S(1)} %maximum_bitcast_fusion), channel_id=2, replica_groups=mesh['dp'=4,'expert'=4,'tensor'=2] {'dp','tensor'}, dimensions={0}, use_global_device_ids=true | all-gather | bytes 62208 | tf_op jit(solution)/shard_map/all_gather | solution.py:241
  99.6 16.7 %collective-permute-done.5 = bf16[4,192,384]{2,1,0:T(8,128)(2,1)} collective-permute-done((bf16[4,192,384]{2,1,0:T(8,128)(2,1)}, bf16[4,192,384]{2,1,0:T(8,128)(2,1)}, u32[]{:S(2)}, u32[]{:S(2)}) %collective-permute-start.5) | collective-permute-done | bytes 589856 | tf_op jit(solution)/shard_map/ppermute | solution.py:47
  175.9 17.3 %all-to-all-done.3 = bf16[4,384,512]{2,1,0:T(8,128)(2,1)} async-done(((bf16[4,384,512]{2,1,0:T(8,128)(2,1)}), bf16[4,384,512]{2,1,0:T(8,128)(2,1)}, u32[]{:S(2)}, u32[]{:S(2)}) %all-to-all-start.3) | async-done | bytes 1572896 | tf_op jit(solution)/shard_map/all_to_all | solution.py:216
  243.9 11.4 %collective-permute-done.33 = bf16[80,1536]{1,0:T(8,128)(2,1)} collective-permute-done((bf16[80,1536]{1,0:T(8,128)(2,1)}, bf16[80,1536]{1,0:T(8,128)(2,1)}, u32[]{:S(2)}, u32[]{:S(2)}) %collective-permute-start.33) | collective-permute-done | bytes 245792 | tf_op jit(solution)/shard_map/ppermute | solution.py:47
  258.0 8.3 collective-permute-done.13
  266.3 6.8 collective-permute-start.11
  276.2 5.3 collective-permute-done.11
  296.5 13.5 %collective-permute-done.63 = bf16[80,1536]{1,0:T(8,128)(2,1)S(1)} collective-permute-done((bf16[80,1536]{1,0:T(8,128)(2,1)S(1)}, bf16[80,1536]{1,0:T(8,128)(2,1)S(1)}, u32[]{:S(2)}, u32[]{:S(2)}) %collective-permute-start.63) | collective-permute-done | bytes 245792 | tf_op jit(solution)/shard_map/ppermute | solution.py:47
  378.2 8.9 %collective-permute-done.66 = bf16[80,1536]{1,0:T(8,128)(2,1)S(1)} collective-permute-done((bf16[80,1536]{1,0:T(8,128)(2,1)S(1)}, bf16[80,1536]{1,0:T(8,128)(2,1)S(1)}, u32[]{:S(2)}, u32[]{:S(2)}) %collective-permute-start.66) | collective-permute-done | bytes 245792 | tf_op jit(solution)/shard_map/ppermute | solution.py:47
  412.7 6.8 collective-permute-done.69
  421.7 6.2 collective-permute-done.52
  472.5 9.5 %collective-permute-done.87 = bf16[4,192,384]{2,1,0:T(8,128)(2,1)S(1)} collective-permute-done((bf16[4,192,384]{2,1,0:T(8,128)(2,1)S(1)}, bf16[4,192,384]{2,1,0:T(8,128)(2,1)S(1)}, u32[]{:S(2)}, u32[]{:S(2)}) %collective-permute-start.87) | collective-permute-done | bytes 589856 | tf_op jit(solution)/shard_map/ppermute | solution.py:47
  482.1 12.1 %collective-permute-done.85 = bf16[4,192,384]{2,1,0:T(8,128)(2,1)S(1)} collective-permute-done((bf16[4,192,384]{2,1,0:T(8,128)(2,1)S(1)}, bf16[4,192,384]{2,1,0:T(8,128)(2,1)S(1)}, u32[]{:S(2)}, u32[]{:S(2)}) %collective-permute-start.85) | collective-permute-done | bytes 589856 | tf_op jit(solution)/shard_map/ppermute | solution.py:47
  517.8 5.9 collective-permute-done.21
  524.3 5.2 all-to-all-start.5
  535.8 109.0 %all-reduce.2.cloned.1.call-done = f32[17,1536]{1,0:T(8,128)} async-done(((f32[17,1536]{1,0:T(8,128)}), f32[17,1536]{1,0:T(8,128)}) %all-reduce.2.cloned.1.call-update) | async-done | bytes 104464 | tf_op jit(solution)/shard_map/psum | solution.py:543
  657.4 6.6 all-to-all-start.9
  673.6 7.6 collective-permute-done.25
  707.7 7.4 collective-permute-done.58
  732.2 40.6 %psum.14 = f32[1536]{0:T(1024)} all-reduce(f32[1536]{0:T(1024)S(1)} %add.469), channel_id=1, replica_groups=mesh['dp'=4,'expert'=4,'tensor'=2] {'dp','expert','tensor'}, use_global_device_ids=true, to_apply=%region_20.21 | all-reduce | flops 1536 | bytes 12288 | tf_op jit(solution)/shard_map/psum | solution.py:545
  787.7 7.6 collective-permute-done.60
  815.9 5.9 collective-permute-done.78
  (683 shorter events, 455.3 us)
Async XLA Ops:
  93.0 59.3 %all-to-all-start.2 = ((bf16[4,384,512]{2,1,0:T(8,128)(2,1)}), bf16[4,384,512]{2,1,0:T(8,128)(2,1)}, u32[]{:S(2)}, u32[]{:S(2)}) async-start(bf16[4,384,512]{2,1,0:T(8,128)(2,1)} %param.28), calls=%async_computation.2 | async-start | bytes 3145728 | tf_op jit(solution)/shard_map/all_to_all | solution.py:216
  169.2 45.5 %collective-permute-start.31 = (bf16[128,1536]{1,0:T(8,128)(2,1)}, bf16[128,1536]{1,0:T(8,128)(2,1)}, u32[]{:S(2)}, u32[]{:S(2)}) collective-permute-start(bf16[128,1536]{1,0:T(8,128)(2,1)} %get-tuple-element.130), channel_id=1, source_target_pairs={{0,6},{2,4},{4,2},{6,0},{1,7},{3,5},{5,3},{7,1},{8,14},{10,12},{12... | collective-permute-start | bytes 1179656 | tf_op jit(solution)/shard_map/ppermute | solution.py:47
  171.5 45.2 %collective-permute-start.29 = (bf16[128,1536]{1,0:T(8,128)(2,1)}, bf16[128,1536]{1,0:T(8,128)(2,1)}, u32[]{:S(2)}, u32[]{:S(2)}) collective-permute-start(bf16[128,1536]{1,0:T(8,128)(2,1)} %get-tuple-element.130), channel_id=1, source_target_pairs={{0,2},{2,0},{4,6},{6,4},{1,3},{3,1},{5,7},{7,5},{8,10},{10,8},{12,... | collective-permute-start | bytes 1179656 | tf_op jit(solution)/shard_map/ppermute | solution.py:47
  193.2 50.6 %all-to-all-start.4 = ((bf16[4,512,384]{1,2,0:T(8,128)(2,1)}), bf16[4,512,384]{1,2,0:T(8,128)(2,1)}, u32[]{:S(2)}, u32[]{:S(2)}) async-start(bf16[4,512,384]{1,2,0:T(8,128)(2,1)} %copy.51), calls=%async_computation.4 | async-start | bytes 3145728 | tf_op jit(solution)/shard_map/all_to_all | solution.py:216
  214.2 67.9 %collective-permute-start.15 = (bf16[1536,512]{1,0:T(8,128)(2,1)}, bf16[1536,512]{1,0:T(8,128)(2,1)}, u32[]{:S(2)}, u32[]{:S(2)}) collective-permute-start(bf16[1536,512]{1,0:T(8,128)(2,1)} %bitcast.37), channel_id=1, source_target_pairs={{0,1},{1,0},{2,3},{3,2},{4,5},{5,4},{6,7},{7,6},{8,9},{9,8},{10,11... | collective-permute-start | bytes 4718600 | tf_op jit(solution)/shard_map/ppermute | solution.py:47
  214.2 74.0 %collective-permute-start.14 = (bf16[1536,512]{1,0:T(8,128)(2,1)}, bf16[1536,512]{1,0:T(8,128)(2,1)}, u32[]{:S(2)}, u32[]{:S(2)}) collective-permute-start(bf16[1536,512]{1,0:T(8,128)(2,1)} %bitcast.36), channel_id=1, source_target_pairs={{0,1},{1,0},{2,3},{3,2},{4,5},{5,4},{6,7},{7,6},{8,9},{9,8},{10,11... | collective-permute-start | bytes 4718600 | tf_op jit(solution)/shard_map/ppermute | solution.py:47
  243.8 69.8 %collective-permute-start.16 = (bf16[512,1536]{0,1:T(8,128)(2,1)}, bf16[512,1536]{0,1:T(8,128)(2,1)S(1)}, u32[]{:S(2)}, u32[]{:S(2)}) collective-permute-start(bf16[512,1536]{0,1:T(8,128)(2,1)} %bitcast.39), channel_id=1, source_target_pairs={{0,1},{1,0},{2,3},{3,2},{4,5},{5,4},{6,7},{7,6},{8,9},{9,8},{10,11... | collective-permute-start | bytes 4718600 | tf_op jit(solution)/shard_map/ppermute | solution.py:47
  276.2 54.2 %collective-permute-start.44 = (bf16[80,1536]{1,0:T(8,128)(2,1)}, bf16[80,1536]{1,0:T(8,128)(2,1)S(1)}, u32[]{:S(2)}, u32[]{:S(2)}) collective-permute-start(bf16[80,1536]{1,0:T(8,128)(2,1)} %convolution_convert_fusion.32), channel_id=1, source_target_pairs={{0,8},{8,0},{16,24},{24,16},{1,9},{9,1},{17,25},{25,17},{2,10},{10... | collective-permute-start | bytes 737288 | tf_op jit(solution)/shard_map/ppermute | solution.py:47
  337.6 63.4 %collective-permute-start.19 = (bf16[80,1536]{1,0:T(8,128)(2,1)S(1)}, bf16[80,1536]{1,0:T(8,128)(2,1)S(1)}, u32[]{:S(2)}, u32[]{:S(2)}) collective-permute-start(bf16[80,1536]{1,0:T(8,128)(2,1)S(1)} %get-tuple-element.81), channel_id=1, source_target_pairs={{0,24},{8,16},{16,8},{24,0},{1,25},{9,17},{17,9},{25,1},{2,26},{10... | collective-permute-start | bytes 737288 | tf_op jit(solution)/shard_map/ppermute | solution.py:47
  337.9 65.0 %collective-permute-start.18 = (bf16[80,1536]{1,0:T(8,128)(2,1)S(1)}, bf16[80,1536]{1,0:T(8,128)(2,1)S(1)}, u32[]{:S(2)}, u32[]{:S(2)}) collective-permute-start(bf16[80,1536]{1,0:T(8,128)(2,1)S(1)} %get-tuple-element.82), channel_id=1, source_target_pairs={{0,16},{8,24},{16,0},{24,8},{1,17},{9,25},{17,1},{25,9},{2,18},{10... | collective-permute-start | bytes 737288 | tf_op jit(solution)/shard_map/ppermute | solution.py:47
  419.5 82.4 %collective-permute-start.37 = (bf16[80,1536]{1,0:T(8,128)(2,1)}, bf16[80,1536]{1,0:T(8,128)(2,1)}, u32[]{:S(2)}, u32[]{:S(2)}) collective-permute-start(bf16[80,1536]{1,0:T(8,128)(2,1)} %get-tuple-element.77), channel_id=1, source_target_pairs={{0,24},{8,16},{16,8},{24,0},{1,25},{9,17},{17,9},{25,1},{2,26},{10... | collective-permute-start | bytes 737288 | tf_op jit(solution)/shard_map/ppermute | solution.py:47
  494.2 157.9 %collective-permute-start.90 = (bf16[512,1536]{1,0:T(8,128)(2,1)}, bf16[512,1536]{1,0:T(8,128)(2,1)}, u32[]{:S(2)}, u32[]{:S(2)}) collective-permute-start(bf16[512,1536]{1,0:T(8,128)(2,1)} %fusion.14), channel_id=1, source_target_pairs={{0,1},{1,0},{2,3},{3,2},{4,5},{5,4},{6,7},{7,6},{8,9},{9,8},{10,11... | collective-permute-start | bytes 4718600 | tf_op jit(solution)/shard_map/ppermute | solution.py:47
  499.4 145.4 %all-reduce.2.cloned.1.call-start = ((), (), s32[]{:S(2)}) async-start(), calls=%async_computation.10 | async-start | bytes 294912 | tf_op jit(solution)/shard_map/psum | solution.py:543
  513.3 185.3 %collective-permute-start.88 = (bf16[1536,512]{1,0:T(8,128)(2,1)}, bf16[1536,512]{1,0:T(8,128)(2,1)}, u32[]{:S(2)}, u32[]{:S(2)}) collective-permute-start(bf16[1536,512]{1,0:T(8,128)(2,1)} %fusion.12), channel_id=1, source_target_pairs={{0,1},{1,0},{2,3},{3,2},{4,5},{5,4},{6,7},{7,6},{8,9},{9,8},{10,11... | collective-permute-start | bytes 4718600 | tf_op jit(solution)/shard_map/ppermute | solution.py:47
  516.4 166.1 %collective-permute-start.40 = (bf16[128,1536]{1,0:T(8,128)(2,1)}, bf16[128,1536]{1,0:T(8,128)(2,1)}, u32[]{:S(2)}, u32[]{:S(2)}) collective-permute-start(bf16[128,1536]{1,0:T(8,128)(2,1)} %convolution_convert_fusion.18), channel_id=1, source_target_pairs={{0,6},{2,4},{4,2},{6,0},{1,7},{3,5},{5,3},{7,1},{8,14},{10,12},{12... | collective-permute-start | bytes 1179656 | tf_op jit(solution)/shard_map/ppermute | solution.py:47
  523.7 160.4 %collective-permute-start.39 = (bf16[128,1536]{1,0:T(8,128)(2,1)}, bf16[128,1536]{1,0:T(8,128)(2,1)}, u32[]{:S(2)}, u32[]{:S(2)}) collective-permute-start(bf16[128,1536]{1,0:T(8,128)(2,1)} %convolution_convert_fusion.19), channel_id=1, source_target_pairs={{0,4},{2,6},{4,0},{6,2},{1,5},{3,7},{5,1},{7,3},{8,12},{10,14},{12... | collective-permute-start | bytes 1179656 | tf_op jit(solution)/shard_map/ppermute | solution.py:47
  524.3 133.1 %all-to-all-start.5 = ((bf16[4,192,640]{2,1,0:T(8,128)(2,1)}), bf16[4,192,640]{2,1,0:T(8,128)(2,1)}, u32[]{:S(2)}, u32[]{:S(2)}) async-start(bf16[4,192,640]{2,1,0:T(8,128)(2,1)} %fusion.43), calls=%async_computation.5 | async-start | bytes 1966080 | tf_op jit(solution)/shard_map/all_to_all | solution.py:507
  534.4 136.9 %collective-permute-start.24 = (bf16[128,1536]{1,0:T(8,128)(2,1)}, bf16[128,1536]{1,0:T(8,128)(2,1)}, u32[]{:S(2)}, u32[]{:S(2)}) collective-permute-start(bf16[128,1536]{1,0:T(8,128)(2,1)} %get-tuple-element.163), channel_id=1, source_target_pairs={{0,4},{2,6},{4,0},{6,2},{1,5},{3,7},{5,1},{7,3},{8,12},{10,14},{12... | collective-permute-start | bytes 1179656 | tf_op jit(solution)/shard_map/ppermute | solution.py:47
  657.4 59.1 %all-to-all-start.9 = ((bf16[4,512,384]{2,1,0:T(8,128)(2,1)}), bf16[4,512,384]{2,1,0:T(8,128)(2,1)}, u32[]{:S(2)}, u32[]{:S(2)}) async-start(bf16[4,512,384]{2,1,0:T(8,128)(2,1)} %bitcast.368), calls=%async_computation.9 | async-start | bytes 3145728 | tf_op jit(solution)/shard_map/all_to_all | solution.py:216
  705.7 90.4 %collective-permute-start.89 = (bf16[1536,512]{1,0:T(8,128)(2,1)}, bf16[1536,512]{1,0:T(8,128)(2,1)}, u32[]{:S(2)}, u32[]{:S(2)}) collective-permute-start(bf16[1536,512]{1,0:T(8,128)(2,1)} %fusion.13), channel_id=1, source_target_pairs={{0,1},{1,0},{2,3},{3,2},{4,5},{5,4},{6,7},{7,6},{8,9},{9,8},{10,11... | collective-permute-start | bytes 4718600 | tf_op jit(solution)/shard_map/ppermute | solution.py:47
  705.7 102.3 %collective-permute-start.42 = (bf16[128,1536]{1,0:T(8,128)(2,1)}, bf16[128,1536]{1,0:T(8,128)(2,1)}, u32[]{:S(2)}, u32[]{:S(2)}) collective-permute-start(bf16[128,1536]{1,0:T(8,128)(2,1)} %get-tuple-element.165), channel_id=1, source_target_pairs={{0,4},{2,6},{4,0},{6,2},{1,5},{3,7},{5,1},{7,3},{8,12},{10,14},{12... | collective-permute-start | bytes 1179656 | tf_op jit(solution)/shard_map/ppermute | solution.py:47
  707.1 70.6 %collective-permute-start.41 = (bf16[128,1536]{1,0:T(8,128)(2,1)}, bf16[128,1536]{1,0:T(8,128)(2,1)}, u32[]{:S(2)}, u32[]{:S(2)}) collective-permute-start(bf16[128,1536]{1,0:T(8,128)(2,1)} %get-tuple-element.165), channel_id=1, source_target_pairs={{0,2},{2,0},{4,6},{6,4},{1,3},{3,1},{5,7},{7,5},{8,10},{10,8},{12,... | collective-permute-start | bytes 1179656 | tf_op jit(solution)/shard_map/ppermute | solution.py:47
  715.1 95.6 %collective-permute-start.43 = (bf16[128,1536]{1,0:T(8,128)(2,1)}, bf16[128,1536]{1,0:T(8,128)(2,1)}, u32[]{:S(2)}, u32[]{:S(2)}) collective-permute-start(bf16[128,1536]{1,0:T(8,128)(2,1)} %get-tuple-element.165), channel_id=1, source_target_pairs={{0,6},{2,4},{4,2},{6,0},{1,7},{3,5},{5,3},{7,1},{8,14},{10,12},{12... | collective-permute-start | bytes 1179656 | tf_op jit(solution)/shard_map/ppermute | solution.py:47
  716.5 83.2 %all-to-all-start.7 = ((bf16[4,384,512]{2,1,0:T(8,128)(2,1)}), bf16[4,384,512]{2,1,0:T(8,128)(2,1)}, u32[]{:S(2)}, u32[]{:S(2)}) async-start(bf16[4,384,512]{2,1,0:T(8,128)(2,1)} %bitcast.369), calls=%async_computation.7 | async-start | bytes 3145728 | tf_op jit(solution)/shard_map/all_to_all | solution.py:216
  (215 other events, 3605.1 us)
Sparse Core Ops, SparseCore 0:
  513.4 131.2 all-reduce.1
